TPU v7x, 32 devices: a whole 2x2x4 slice. The times are simulated.
32 devices in a mesh: groups: 2 (over y), blk: 4 (over z), dp: 2 (over x), sub: 2 (over core).
Axes of the slice: x: 2, y: 2, z: 4, core: 2. Of those that a mesh axis runs over, the one named last changes fastest.
Arguments:
- view_a: bfloat16 [2048, 256], P(('groups', 'blk', 'dp', 'sub')), parts along dimension 0, may hold values from -6 to 6
- view_b: bfloat16 [2048, 256], P(('groups', 'blk', 'dp', 'sub')), parts along dimension 0, may hold values from -6 to 6
- prototypes: bfloat16 [32768, 256], P('blk'), may hold values from -6 to 6
- tile_mask: int32 [16, 256], replicated, may hold values from 0 to 1, as said below
- tile_region: int32 [32], P('groups'), parts along dimension 0, may hold values from 0 to 15, as said below
Outputs:
- grad_view_b: float32 [2048, 256], P(('groups', 'blk', 'dp', 'sub')), parts along dimension 0
- grad_prototypes: float32 [65536, 256], P(('groups', 'blk', 'dp', 'sub')), parts along dimension 0
There are 2 independent parts, one for each index of `groups`. A program takes and returns all parts, laid end to end along the dimension named above; an argument that names none is the same for every part. Nothing has to cross between parts.
Inputs may be any that keep to these rules, and one draw needn't show every extreme that they name: `tile_mask`: every prototype tile is 1 for at least one region, and every region for at least 16 tiles. `tile_region`: every region is named by at least one hit tile.
All inputs are finite; a program needn't handle non-finite values.
Results may differ from a plain program's by a relative error of at most 0.00045.
The roundings to bfloat16 on the way count: a program that leaves them out, or rounds other values in their place, can miss the bound.
Values may be sent and summed in bfloat16 or wider, within the bound.
A program may use at most 64 MiB of HBM per device.

v0:
```python
import jax
import jax.numpy as jnp
from jax import lax
from jax.sharding import PartitionSpec as P

TILE = 128
ITERS = 3
SOFTMAX_TEMPER = 0.1
EPSILON = 0.05
PART = ("blk", "dp", "sub")


def unit_rows(matrix):
    values = matrix.astype(jnp.float32)
    return (values * lax.rsqrt(jnp.sum(values * values, axis=1, keepdims=True) + 1e-06)).astype(
        jnp.bfloat16
    )


def body(view_a, view_b, prototypes, tile_mask, tile_region):
    n_dp = lax.axis_size("dp")
    n_sub = lax.axis_size("sub")
    blk_pos = lax.axis_index("blk")
    inner_pos = lax.axis_index("dp") * n_sub + lax.axis_index("sub")
    hit_dev, width = view_a.shape
    cols = prototypes.shape[0] // (n_dp * n_sub)
    tiles = cols // TILE
    regions = tile_mask.shape[0]
    protos = unit_rows(lax.dynamic_slice_in_dim(prototypes, inner_pos * cols, cols, 0))
    both = jnp.concatenate([unit_rows(view_a), unit_rows(view_b)], axis=1)
    both = lax.all_gather(both, PART, axis=0, tiled=True)
    rows_a, rows_b = (both[:, :width], both[:, width:])
    hits = rows_a.shape[0]
    own_tile = (blk_pos * n_dp * n_sub + inner_pos) * tiles
    my_mask = lax.dynamic_slice_in_dim(tile_mask, own_tile, tiles, 1).astype(jnp.float32)
    onehot = (tile_region[:, None] == jnp.arange(regions, dtype=jnp.int32)[None, :]).astype(
        jnp.float32
    )
    flags = jnp.dot(onehot, my_mask) > 0.5
    active = jnp.broadcast_to(
        flags[:, None, :, None], (hits // hit_dev, hit_dev, tiles, TILE)
    ).reshape(hits, cols)

    def scores(rows):
        return jnp.einsum("rd,kd->rk", rows, protos, preferred_element_type=jnp.float32)

    code_exp = jnp.where(active, jnp.exp((scores(rows_a) - 1.0) / EPSILON), 0.0).astype(
        jnp.bfloat16
    )
    pred = jnp.where(active, jnp.exp((scores(rows_b) - 1.0) / SOFTMAX_TEMPER), 0.0)
    norm = jnp.sum(pred, axis=1)
    code = code_exp.astype(jnp.float32)
    row = jnp.ones((hits,), jnp.float32)
    for sweep in range(ITERS):
        col = 1.0 / jnp.sum(code * row[:, None], axis=0)
        part = jnp.sum(code * col[None, :], axis=1)
        if sweep == 0:
            part, norm = lax.psum((part, norm), PART)
        else:
            part = lax.psum(part, PART)
        row = 1.0 / part
    grad = ((pred / norm[:, None] - row[:, None] * code * col[None, :]) / SOFTMAX_TEMPER).astype(
        jnp.bfloat16
    )
    hit_part = jnp.dot(grad, protos, preferred_element_type=jnp.float32)
    grad_protos = jnp.einsum("rk,rd->kd", grad, rows_b, preferred_element_type=jnp.float32)
    return (lax.psum_scatter(hit_part, PART, scatter_dimension=0, tiled=True), grad_protos)


def solution(mesh):
    spread = P(("groups", "blk", "dp", "sub"), None)
    return jax.shard_map(
        body,
        mesh=mesh,
        in_specs=(spread, spread, P("blk", None), P(), P("groups")),
        out_specs=(spread, spread),
        check_vma=False,
    )
```

profile of v0, /device:TPU:0, one launch (start us, length us, event | category | flops | bytes accessed | tf_op | source)
XLA Modules:
  0.0 244.8 jit_solution(6231227928295905269)
XLA Ops:
  7.2 0.0 all-gather.2.cloned.1.call-start
  7.2 0.9 fusion.17
  8.1 0.9 fusion.19
  9.0 0.9 fusion.18
  9.9 0.6 pad_maximum_fusion
  10.5 0.0 all-gather.2.cloned.1.call-update
  10.5 0.0 reduce-scatter.2.cloned.1.call-start
  10.6 1.6 fusion.10
  12.2 0.9 convolution_compare_fusion
  13.1 38.3 %all-gather.2.cloned.1.call-done = bf16[1024,512]{1,0:T(8,128)(2,1)} async-done(((bf16[64,512]{1,0:T(8,128)(2,1)}), bf16[1024,512]{1,0:T(8,128)(2,1)}) %all-gather.2.cloned.1.call-update) | async-done | bytes 1048592 | tf_op jit(solution)/shard_map/all_gather | solution.py:31
  51.4 0.6 broadcast_in_dim.6
  52.0 4.3 %convert_reduce_fusion = (f32[2048]{0:T(1024)S(1)}, bf16[1024,2048]{1,0:T(8,128)(2,1)S(1)}) fusion(f32[2048]{0:T(1024)S(1)} %add_rsqrt_fusion, bf16[8192,256]{1,0:T(8,128)(2,1)} %param.7, s32[]{:T(128)S(6)} %select_n.14, bf16[1024,512]{1,0:T(8,128)(2,1)} %all-gather.2.cloned.1.call-done, pred[128,8,16,128]{3,2,1,0:T(8,128)(4,1)S(1)} %bitcast.11), kind=kOutput, calls=%fused_computation.6 | convolution fusion | flops 1087895552 | bytes 7880708 | tf_op jit(solution)/shard_map/rd,kd->rk/dot_general | solution.py:45
  56.3 0.0 copy-start
  56.4 2.0 copy-done
  58.3 0.9 fusion
  59.2 31.6 %psum.29 = f32[1024]{0:T(1024)S(1)} all-reduce(f32[1024]{0:T(1024)S(1)} %fusion), channel_id=1, replica_groups=mesh['groups'=2,'blk'=4,'dp'=2,'sub'=2] {'blk','dp','sub'}, use_global_device_ids=true, to_apply=%region_7.8 | all-reduce | flops 1024 | bytes 8192 | tf_op jit(solution)/shard_map/psum | solution.py:58
  90.8 0.0 copy-start.2
  90.8 3.2 %fusion.1 = f32[2048]{0:T(1024)S(1)} fusion(bf16[1024,2048]{1,0:T(8,128)(2,1)} %copy-done, f32[1024]{0:T(1024)S(1)} %broadcast_divide_fusion.5), kind=kLoop, calls=%fused_computation.8 | loop fusion | flops 6289408 | bytes 4206592 | tf_op jit(solution)/shard_map/reduce_sum | solution.py:55
  94.0 3.1 %fusion.2 = f32[1024]{0:T(1024)S(1)} fusion(bf16[1024,2048]{1,0:T(8,128)(2,1)} %copy-done, f32[2048]{0:T(1024)S(1)} %broadcast_divide_fusion.1), kind=kLoop, calls=%fused_computation.9 | loop fusion | flops 6290432 | bytes 4206592 | tf_op jit(solution)/shard_map/reduce_sum | solution.py:56
  97.1 29.7 %psum.30 = f32[1024]{0:T(1024)S(1)} all-reduce(f32[1024]{0:T(1024)S(1)} %fusion.2), channel_id=1, replica_groups=mesh['groups'=2,'blk'=4,'dp'=2,'sub'=2] {'blk','dp','sub'}, use_global_device_ids=true, to_apply=%region_10.11 | all-reduce | flops 1024 | bytes 8192 | tf_op jit(solution)/shard_map/psum | solution.py:60
  126.8 3.1 %fusion.3 = f32[2048]{0:T(1024)S(1)} fusion(bf16[1024,2048]{1,0:T(8,128)(2,1)} %copy-done, f32[1024]{0:T(1024)S(1)} %broadcast_divide_fusion.4), kind=kLoop, calls=%fused_computation.10 | loop fusion | flops 6289408 | bytes 4206592 | tf_op jit(solution)/shard_map/reduce_sum | solution.py:55
  129.9 3.1 %fusion.4 = f32[1024]{0:T(1024)S(1)} fusion(bf16[1024,2048]{1,0:T(8,128)(2,1)} %copy-done, f32[2048]{0:T(1024)S(1)} %broadcast_divide_fusion), kind=kLoop, calls=%fused_computation.11 | loop fusion | flops 6290432 | bytes 4206592 | tf_op jit(solution)/shard_map/reduce_sum | solution.py:56
  132.9 0.0 copy-done.2
  132.9 7.3 %fusion.9 = (f32[1024]{0:T(1024)S(1)}, f32[1024,2048]{1,0:T(8,128)}) fusion(pred[128,8,16,128]{3,2,1,0:T(8,128)(4,1)S(1)} %bitcast.12, f32[2048]{0:T(1024)S(1)} %add_rsqrt_fusion, bf16[8192,256]{1,0:T(8,128)(2,1)} %param.7, s32[]{:T(128)S(6)} %select_n.14, bf16[1024,512]{1,0:T(8,128)(2,1)S(1)} %copy-done.2), kind=kOutput, calls=%fused_computation.18 | convolution fusion | flops 1083702272 | bytes 12070916 | tf_op jit(solution)/shard_map/rd,kd->rk/dot_general | solution.py:45
  140.2 30.0 %all-reduce = (f32[1024]{0:T(1024)S(1)}, f32[1024]{0:T(1024)S(1)}) all-reduce(f32[1024]{0:T(1024)S(1)} %fusion.4, f32[1024]{0:T(1024)S(1)} %get-tuple-element.6), channel_id=1, replica_groups=mesh['groups'=2,'blk'=4,'dp'=2,'sub'=2] {'blk','dp','sub'}, use_global_device_ids=true, to_apply=%region_13.14 | all-reduce | flops 2048 | bytes 16384 | tf_op jit(solution)/shard_map/psum | solution.py:60
  170.2 7.4 %fusion.8 = bf16[1024,2048]{1,0:T(8,128)(2,1)S(1)} fusion(bf16[1024,2048]{1,0:T(8,128)(2,1)} %copy-done, f32[1024,2048]{1,0:T(8,128)} %get-tuple-element.7, pred[128,8,16,128]{3,2,1,0:T(8,128)(4,1)S(1)} %bitcast.13, f32[1024]{0:T(1024)S(1)} %broadcast_divide_fusion.3, f32[2048]{0:T(1024)S(1)} %broadcast_divide_fusion, f32[1024]{0:T(1024)S(1)} %get-tuple-element.3), kind=kLoop, calls=%fused_computation.15 | loop fusion | flops 20971520 | bytes 18890752 | tf_op jit(solution)/shard_map/convert_element_type | solution.py:62
  177.6 0.0 copy-start.1
  177.7 1.9 copy-done.1
  179.6 3.6 %fusion.25 = f32[1024,256]{1,0:T(8,128)} fusion(bf16[1024,2048]{1,0:T(8,128)(2,1)S(1)} %fusion.8, f32[2048]{0:T(1024)S(1)} %add_rsqrt_fusion, bf16[8192,256]{1,0:T(8,128)(2,1)} %param.7, s32[]{:T(128)S(6)} %select_n.14), kind=kOutput, calls=%fused_computation.52 | convolution fusion | flops 1075314688 | bytes 6299652 | tf_op jit(solution)/shard_map/dot_general | solution.py:65
  183.1 0.0 reduce-scatter.2.cloned.1.call-update
  183.2 4.8 %fusion.13 = f32[2048,256]{1,0:T(8,128)} fusion(bf16[1024,2048]{1,0:T(8,128)(2,1)} %copy-done.1, bf16[1024,512]{1,0:T(8,128)(2,1)S(1)} %copy-done.2), kind=kOutput, calls=%fused_computation.25 | convolution fusion | flops 1073741824 | bytes 6815744 | tf_op jit(solution)/shard_map/rk,rd->kd/dot_general | solution.py:66
  188.0 49.9 %reduce-scatter.2.cloned.1.call-done = f32[64,256]{1,0:T(8,128)} async-done(((f32[1024,256]{1,0:T(8,128)}), f32[64,256]{1,0:T(8,128)}) %reduce-scatter.2.cloned.1.call-update) | async-done | bytes 65552 | tf_op jit(solution)/shard_map/reduce_scatter | solution.py:67
  (9 shorter events, 0.0 us)
Async XLA Ops:
  7.2 44.2 %all-gather.2.cloned.1.call-start = ((), (), s32[]{:S(2)}) async-start(), calls=%async_computation.1 | async-start | bytes 1114112 | tf_op jit(solution)/shard_map/all_gather | solution.py:31
  10.5 227.4 %reduce-scatter.2.cloned.1.call-start = ((), (), s32[]{:S(2)}) async-start(), calls=%async_computation.2 | async-start | bytes 1114112 | tf_op jit(solution)/shard_map/reduce_scatter | solution.py:67
  56.3 2.0 copy-start
  90.8 42.1 %copy-start.2 = (bf16[1024,512]{1,0:T(8,128)(2,1)S(1)}, bf16[1024,512]{1,0:T(8,128)(2,1)}, u32[]{:S(2)}) copy-start(bf16[1024,512]{1,0:T(8,128)(2,1)} %all-gather.2.cloned.1.call-done) | copy-start | bytes 3145732
  177.6 1.9 copy-start.1
Sparse Core Ops, SparseCore 0:
  10.7 40.6 all-gather.1
  183.3 54.6 reduce-scatter.1
where the time goes:
time: 245 us
  blocking collectives  91.2 us (37%)
  waiting for transfers between devices  88.3 us (36%)
  other arithmetic  25.6 us (10%)
  matrix products  20.9 us (9%)
  between operations  14.2 us (6%)
  local copies, waits for them, and re-layouts  4.48 us (2%)
    psum x2, blocking collectives, body(): part = lax.psum(part, PART)  59.6 us
    reduce_scatter x1, waiting for transfers between devices, body(): lax.psum_scatter(hit_part, PART, scatter_dimension=0, tiled=True)  49.9 us
    all_gather x1, waiting for transfers between devices, body(): both = lax.all_gather(both, PART, axis=0, tiled=True)  38.3 us
    psum x1, blocking collectives, body(): part, norm = lax.psum((part, norm), PART)  31.6 us
    dot_general x2, matrix products, scores(): jnp.einsum('rd,kd->rk', rows, protos, preferred_element_type=jnp.float32)  11.6 us
    convert_element_type x1, other arithmetic, body(): ((pred / norm[:, None] - row[:, None] * code * col[None, :]) / SOFTMAX_TE...  7.44 us
    reduce_sum x3, other arithmetic, body(): part = jnp.sum(code * col[None, :], axis=1)  7.06 us
    reduce_sum x2, other arithmetic, body(): col = 1.0 / jnp.sum(code * row[:, None], axis=0)  6.24 us
  transfers between devices with their start and end apart: 2, of which 2 were waited for; matrix products, arithmetic and copies ran while one was open for 3% of the time, Pallas kernels for 0%

commit v1 on v0

--- a/solution.py
+++ b/solution.py
@@ -57,7 +57,7 @@
         if sweep == 0:
             part, norm = lax.psum((part, norm), PART)
         else:
-            part = lax.psum(part, PART)
+            part = jnp.sum(lax.all_gather(part, PART), axis=0)
         row = 1.0 / part
     grad = ((pred / norm[:, None] - row[:, None] * code * col[None, :]) / SOFTMAX_TEMPER).astype(
         jnp.bfloat16

time: 245 us -> 222 us (0.906)
  blocking collectives: 91.2 us -> 68.8 us
    psum x2 -> x0, blocking collectives: 59.6 us -> none  [body(): part = lax.psum(part, PART)]
    all_gather x0 -> x2, blocking collectives: none -> 36.7 us  [body(): part = jnp.sum(lax.all_gather(part, PART), axis=0)]
where the time goes in v1:
time: 222 us; the launch traced here: 221 us
  waiting for transfers between devices  88.3 us (40%)
  blocking collectives  68.8 us (31%)
  other arithmetic  25.5 us (11%)
  matrix products  21.5 us (10%)
  between operations  14.2 us (6%)
  local copies, waits for them, and re-layouts  2.57 us (1%)
    reduce_scatter x1, waiting for transfers between devices, body(): lax.psum_scatter(hit_part, PART, scatter_dimension=0, tiled=True)  49.9 us
    all_gather x1, waiting for transfers between devices, body(): both = lax.all_gather(both, PART, axis=0, tiled=True)  38.3 us
    all_gather x2, blocking collectives, body(): part = jnp.sum(lax.all_gather(part, PART), axis=0)  36.7 us
    psum x1, blocking collectives, body(): part, norm = lax.psum((part, norm), PART)  32.1 us
    dot_general x2, matrix products, scores(): jnp.einsum('rd,kd->rk', rows, protos, preferred_element_type=jnp.float32)  12.2 us
    convert_element_type x1, other arithmetic, body(): ((pred / norm[:, None] - row[:, None] * code * col[None, :]) / SOFTMAX_TE...  7.44 us
    reduce_sum x3, other arithmetic, body(): part = jnp.sum(code * col[None, :], axis=1)  7.06 us
    reduce_sum x2, other arithmetic, body(): col = 1.0 / jnp.sum(code * row[:, None], axis=0)  6.15 us
  transfers between devices with their start and end apart: 2, of which 2 were waited for; matrix products, arithmetic and copies ran while one was open for 3% of the time, Pallas kernels for 0%

profile of v1, /device:TPU:0, one launch (start us, length us, event | category | flops | bytes accessed | tf_op | source)
XLA Modules:
  0.0 221.1 jit_solution(14893754254461348553)
XLA Ops:
  7.2 0.0 all-gather.4.cloned.1.call-start
  7.2 0.9 fusion.17
  8.1 0.9 fusion.19
  9.0 0.9 fusion.18
  9.9 0.6 pad_maximum_fusion
  10.5 0.0 all-gather.4.cloned.1.call-update
  10.5 0.0 reduce-scatter.2.cloned.1.call-start
  10.6 1.6 fusion.10
  12.2 0.9 convolution_compare_fusion
  13.1 38.3 %all-gather.4.cloned.1.call-done = bf16[1024,512]{1,0:T(8,128)(2,1)} async-done(((bf16[64,512]{1,0:T(8,128)(2,1)}), bf16[1024,512]{1,0:T(8,128)(2,1)}) %all-gather.4.cloned.1.call-update) | async-done | bytes 1048592 | tf_op jit(solution)/shard_map/all_gather | solution.py:31
  51.4 0.6 broadcast_in_dim.6
  52.0 0.0 copy-start.2
  52.0 4.4 %convert_reduce_fusion = (f32[2048]{0:T(1024)S(1)}, bf16[1024,2048]{1,0:T(8,128)(2,1)S(1)}) fusion(f32[2048]{0:T(1024)S(1)} %add_rsqrt_fusion, bf16[8192,256]{1,0:T(8,128)(2,1)} %param.7, s32[]{:T(128)S(6)} %select_n.14, bf16[1024,512]{1,0:T(8,128)(2,1)} %all-gather.4.cloned.1.call-done, pred[128,8,16,128]{3,2,1,0:T(8,128)(4,1)S(1)} %bitcast.11), kind=kOutput, calls=%fused_computation.6 | convolution fusion | flops 1087895552 | bytes 7880708 | tf_op jit(solution)/shard_map/rd,kd->rk/dot_general | solution.py:45
  56.4 0.0 copy-start
  56.5 0.9 fusion
  57.4 0.0 copy-done.2
  57.4 7.8 %fusion.9 = (f32[1024]{0:T(1024)S(1)}, f32[1024,2048]{1,0:T(8,128)}) fusion(pred[128,8,16,128]{3,2,1,0:T(8,128)(4,1)S(1)} %bitcast.12, f32[2048]{0:T(1024)S(1)} %add_rsqrt_fusion, bf16[8192,256]{1,0:T(8,128)(2,1)} %param.7, s32[]{:T(128)S(6)} %select_n.14, bf16[1024,512]{1,0:T(8,128)(2,1)S(1)} %copy-done.2), kind=kOutput, calls=%fused_computation.18 | convolution fusion | flops 1083702272 | bytes 12070916 | tf_op jit(solution)/shard_map/rd,kd->rk/dot_general | solution.py:45
  65.2 0.0 copy-done
  65.2 32.1 %all-reduce = (f32[1024]{0:T(1024)S(1)}, f32[1024]{0:T(1024)S(1)}) all-reduce(f32[1024]{0:T(1024)S(1)} %fusion, f32[1024]{0:T(1024)S(1)} %get-tuple-element.6), channel_id=1, replica_groups=mesh['groups'=2,'blk'=4,'dp'=2,'sub'=2] {'blk','dp','sub'}, use_global_device_ids=true, to_apply=%region_7.8 | all-reduce | flops 2048 | bytes 16384 | tf_op jit(solution)/shard_map/psum | solution.py:58
  97.3 3.1 %fusion.1 = f32[2048]{0:T(1024)S(1)} fusion(bf16[1024,2048]{1,0:T(8,128)(2,1)} %copy-done, f32[1024]{0:T(1024)S(1)} %broadcast_divide_fusion.5), kind=kLoop, calls=%fused_computation.8 | loop fusion | flops 6289408 | bytes 4206592 | tf_op jit(solution)/shard_map/reduce_sum | solution.py:55
  100.4 3.1 %fusion.2 = f32[1024]{0:T(1024)S(1)} fusion(bf16[1024,2048]{1,0:T(8,128)(2,1)} %copy-done, f32[2048]{0:T(1024)S(1)} %broadcast_divide_fusion.1), kind=kLoop, calls=%fused_computation.9 | loop fusion | flops 6290432 | bytes 4206592 | tf_op jit(solution)/shard_map/reduce_sum | solution.py:56
  103.4 17.5 %all-gather = f32[16384]{0:T(1024)S(1)} all-gather(f32[1024]{0:T(1024)S(1)} %fusion.2), channel_id=2, replica_groups=mesh['groups'=2,'blk'=4,'dp'=2,'sub'=2] {'blk','dp','sub'}, dimensions={0}, use_global_device_ids=true | all-gather | bytes 69632 | tf_op jit(solution)/shard_map/all_gather | solution.py:60
  121.0 3.1 %fusion.3 = f32[2048]{0:T(1024)S(1)} fusion(bf16[1024,2048]{1,0:T(8,128)(2,1)} %copy-done, f32[1024]{0:T(1024)S(1)} %broadcast_divide_fusion.4), kind=kLoop, calls=%fused_computation.10 | loop fusion | flops 6289408 | bytes 4206592 | tf_op jit(solution)/shard_map/reduce_sum | solution.py:55
  124.1 3.1 %fusion.4 = f32[1024]{0:T(1024)S(1)} fusion(bf16[1024,2048]{1,0:T(8,128)(2,1)} %copy-done, f32[2048]{0:T(1024)S(1)} %broadcast_divide_fusion), kind=kLoop, calls=%fused_computation.11 | loop fusion | flops 6290432 | bytes 4206592 | tf_op jit(solution)/shard_map/reduce_sum | solution.py:56
  127.1 19.2 %all-gather.1 = f32[16384]{0:T(1024)S(1)} all-gather(f32[1024]{0:T(1024)S(1)} %fusion.4), channel_id=3, replica_groups=mesh['groups'=2,'blk'=4,'dp'=2,'sub'=2] {'blk','dp','sub'}, dimensions={0}, use_global_device_ids=true | all-gather | bytes 69632 | tf_op jit(solution)/shard_map/all_gather | solution.py:60
  146.4 7.4 %fusion.8 = bf16[1024,2048]{1,0:T(8,128)(2,1)S(1)} fusion(bf16[1024,2048]{1,0:T(8,128)(2,1)} %copy-done, f32[1024,2048]{1,0:T(8,128)} %get-tuple-element.7, pred[128,8,16,128]{3,2,1,0:T(8,128)(4,1)S(1)} %bitcast.13, f32[1024]{0:T(1024)S(1)} %broadcast_divide_fusion.3, f32[2048]{0:T(1024)S(1)} %broadcast_divide_fusion, f32[1024]{0:T(1024)S(1)} %get-tuple-element.3), kind=kLoop, calls=%fused_computation.15 | loop fusion | flops 20971520 | bytes 18890752 | tf_op jit(solution)/shard_map/convert_element_type | solution.py:62
  153.9 0.0 copy-start.1
  153.9 1.9 copy-done.1
  155.8 3.6 %fusion.25 = f32[1024,256]{1,0:T(8,128)} fusion(bf16[1024,2048]{1,0:T(8,128)(2,1)S(1)} %fusion.8, f32[2048]{0:T(1024)S(1)} %add_rsqrt_fusion, bf16[8192,256]{1,0:T(8,128)(2,1)} %param.7, s32[]{:T(128)S(6)} %select_n.14), kind=kOutput, calls=%fused_computation.52 | convolution fusion | flops 1075314688 | bytes 6299652 | tf_op jit(solution)/shard_map/dot_general | solution.py:65
  159.4 0.0 reduce-scatter.2.cloned.1.call-update
  159.4 4.9 %fusion.13 = f32[2048,256]{1,0:T(8,128)} fusion(bf16[1024,2048]{1,0:T(8,128)(2,1)} %copy-done.1, bf16[1024,512]{1,0:T(8,128)(2,1)S(1)} %copy-done.2), kind=kOutput, calls=%fused_computation.25 | convolution fusion | flops 1073741824 | bytes 6815744 | tf_op jit(solution)/shard_map/rk,rd->kd/dot_general | solution.py:66
  164.3 49.9 %reduce-scatter.2.cloned.1.call-done = f32[64,256]{1,0:T(8,128)} async-done(((f32[1024,256]{1,0:T(8,128)}), f32[64,256]{1,0:T(8,128)}) %reduce-scatter.2.cloned.1.call-update) | async-done | bytes 65552 | tf_op jit(solution)/shard_map/reduce_scatter | solution.py:67
  (13 shorter events, 0.1 us)
Async XLA Ops:
  7.2 44.2 %all-gather.4.cloned.1.call-start = ((), (), s32[]{:S(2)}) async-start(), calls=%async_computation.1 | async-start | bytes 1114112 | tf_op jit(solution)/shard_map/all_gather | solution.py:31
  10.5 203.7 %reduce-scatter.2.cloned.1.call-start = ((), (), s32[]{:S(2)}) async-start(), calls=%async_computation.2 | async-start | bytes 1114112 | tf_op jit(solution)/shard_map/reduce_scatter | solution.py:67
  52.0 5.3 %copy-start.2 = (bf16[1024,512]{1,0:T(8,128)(2,1)S(1)}, bf16[1024,512]{1,0:T(8,128)(2,1)}, u32[]{:S(2)}) copy-start(bf16[1024,512]{1,0:T(8,128)(2,1)} %all-gather.4.cloned.1.call-done) | copy-start | bytes 3145732
  56.4 8.7 %copy-start = (bf16[1024,2048]{1,0:T(8,128)(2,1)}, bf16[1024,2048]{1,0:T(8,128)(2,1)S(1)}, u32[]{:S(2)}) copy-start(bf16[1024,2048]{1,0:T(8,128)(2,1)S(1)} %get-tuple-element.5) | copy-start | bytes 12582916
  153.9 1.9 copy-start.1
Sparse Core Ops, SparseCore 0:
  10.7 40.6 all-gather.3
  159.5 54.6 reduce-scatter.1
